TPU v7x, 32 devices: a whole 2x2x4 slice. The times are simulated.
32 devices in a mesh: emit: 4 (over z), elem: 8 (over y, x, core).
Axes of the slice: x: 2, y: 2, z: 4, core: 2. Of those that a mesh axis runs over, the one named last changes fastest.
Arguments:
- traces: float32 [256, 1024, 1024], P('emit', 'elem'), may hold values from -6 to 6
- codes: float32 [4, 2, 128], replicated, may hold values from -0.5 to 0.5
- code_of: int32 [256], replicated, may hold values from 0 to 3
- order: int32 [256], replicated, may hold values from 0 to 255, each once
- steer: float32 [256, 1024, 256], P(None, 'elem'), may hold values from -0.1875 to 0.1875
Outputs:
- beams: float32 [256, 256, 256], P('elem', 'emit')
Inputs may be any that keep to these rules, and one draw needn't show every extreme that they name: `order`: each value 0 to 255 appears exactly once.
All inputs are finite; a program needn't handle non-finite values.
Results may differ from a plain program's by a relative error of at most 0.000071.
Values sent between devices are 32-bit elements; how exact they have to be, the bound alone decides.
No kernel may reach another device: no remote copies, remote signals or barrier semaphores. Data moves between devices by JAX's collectives and lax.ppermute only.
A program may use at most 320 MiB of HBM per device.

v0:
```python
import jax
import jax.numpy as jnp
from jax import lax
from jax.sharding import PartitionSpec as P


def toeplitz_table(codes):
    taps = codes.shape[2]
    rows = jnp.arange(2 * taps, dtype=jnp.int32)[:, None]
    cols = jnp.arange(taps, dtype=jnp.int32)[None, :]
    offset = rows - cols
    inside = (offset >= 0) & (offset < taps)
    clipped = jnp.clip(offset, 0, taps - 1)
    in_phase = jnp.where(inside[None], codes[:, 0, :][:, clipped], 0.0)
    quadrature = jnp.where(inside[None], codes[:, 1, :][:, clipped], 0.0)
    return jnp.concatenate([in_phase, quadrature], axis=2)


def hadamard_signs(order, columns, emissions):
    parity = jnp.zeros((order.shape[0], columns.shape[0]), jnp.int32)
    for bit in range(emissions.bit_length()):
        parity = parity + (order[:, None] >> bit & columns[None, :] >> bit & 1)
    signs = (1 - 2 * (parity % 2)).astype(jnp.float32)
    return signs / jnp.sqrt(jnp.float32(emissions))


def spectral_table(samples, taps, bins):
    rows = jnp.arange(samples // taps * 2 * taps, dtype=jnp.int32)
    block = rows // (2 * taps)
    quad = rows // taps % 2
    sample = block * taps + rows % taps
    freqs = jnp.arange(bins, dtype=jnp.int32) - bins // 2
    phase = jnp.mod(sample[:, None] * freqs[None, :], samples).astype(jnp.float32)
    angle = phase * (2.0 * jnp.pi / samples)
    cosine = jnp.cos(angle)
    sine = jnp.sin(angle)
    is_quad = quad[:, None] == 1
    real_cols = jnp.where(is_quad, sine, cosine)
    imag_cols = jnp.where(is_quad, cosine, -sine)
    return jnp.concatenate([real_cols, imag_cols], axis=1) / jnp.sqrt(jnp.float32(samples))


def steer_bins(source, steer, count, contract):
    bins = steer.shape[0]
    half = steer.shape[2] // 2
    real_part = lax.slice_in_dim(source, 0, count, axis=0)
    imag_part = lax.dynamic_slice_in_dim(source, bins, count, 0)
    numbers = (((contract,), (1,)), ((0,), (0,)))
    first = lax.dot_general(real_part, steer, numbers, precision=lax.Precision.HIGHEST)
    second = lax.dot_general(imag_part, steer, numbers, precision=lax.Precision.HIGHEST)
    return jnp.concatenate(
        [first[..., :half] - second[..., half:], first[..., half:] + second[..., :half]], axis=2
    )


def per_device(traces, codes, code_of, order, steer):
    edev, mdev, samples = traces.shape
    ncode, taps = (codes.shape[0], codes.shape[2])
    emissions = order.shape[0]
    bins = steer.shape[0]
    bins_dev = bins // lax.axis_size("elem")
    nblock = samples // taps
    first = lax.axis_index("emit") * edev
    own_codes = lax.dynamic_slice_in_dim(code_of, first, edev)
    onehot = (own_codes[:, None] == jnp.arange(ncode, dtype=jnp.int32)[None, :]).astype(jnp.float32)
    table = toeplitz_table(codes)
    picked = jnp.einsum("ec,cjd->ejd", onehot, table, precision=lax.Precision.HIGHEST)
    blocks = traces.reshape(edev, mdev, nblock, taps)
    current = jnp.einsum(
        "emnj,ejd->emnd", blocks, picked[:, :taps, :], precision=lax.Precision.HIGHEST
    )
    following = jnp.einsum(
        "emnj,ejd->emnd", blocks, picked[:, taps:, :], precision=lax.Precision.HIGHEST
    )
    following = jnp.concatenate(
        [following[:, :, 1:], jnp.zeros((edev, mdev, 1, 2 * taps), jnp.float32)], axis=2
    )
    corr = (current + following).reshape(edev, mdev, nblock * 2 * taps)
    transform = spectral_table(samples, taps, bins)
    spectra = lax.dot_general(
        transform, corr, (((0,), (2,)), ((), ())), precision=lax.Precision.HIGHEST
    )
    columns = first + jnp.arange(edev, dtype=jnp.int32)
    hadamard = hadamard_signs(order, columns, emissions)
    coded = lax.psum_scatter(
        steer_bins(spectra, steer, bins_dev * lax.axis_size("elem"), 2),
        "elem",
        scatter_dimension=0,
        tiled=True,
    )
    folded = lax.dot_general(
        lax.all_gather(coded, "emit", axis=1, tiled=True),
        hadamard,
        (((1,), (0,)), ((), ())),
        precision=lax.Precision.HIGHEST,
    )
    beams = jnp.transpose(folded, (0, 2, 1))
    return beams


def solution(mesh):
    placed = (P("emit", "elem", None), P(), P(), P(), P(None, "elem", None))
    return jax.shard_map(
        per_device, mesh=mesh, in_specs=placed, out_specs=P("elem", "emit", None), check_vma=False
    )
```

profile of v0, /device:TPU:0, one launch (start us, length us, event | category | flops | bytes accessed | tf_op | source)
XLA Modules:
  0.0 971.7 jit_solution(796748638702718246)
XLA Ops:
  6.5 0.0 reduce-scatter.2.cloned.1.call-start
  6.5 0.1 fusion.34
  6.7 0.8 fusion.103
  7.5 0.1 copy.39
  7.6 109.0 %gather_fusion = f32[32768,4]{1,0:T(8,128)} fusion(f32[4,128]{0,1:T(8,128)S(1)} %bitcast.66, s32[32768]{0:T(1024)S(1)} %fusion.34), kind=kCustom, calls=%fused_computation | custom fusion | bytes 1179648 | tf_op jit(solution)/shard_map/gather | solution.py:14
  116.5 9.4 copy.17
  126.0 0.1 copy.40
  126.1 109.0 %gather_fusion.1 = f32[32768,4]{1,0:T(8,128)} fusion(f32[4,128]{0,1:T(8,128)S(1)} %bitcast.65, s32[32768]{0:T(1024)S(1)} %fusion.34), kind=kCustom, calls=%fused_computation.1 | custom fusion | bytes 1179648 | tf_op jit(solution)/shard_map/gather | solution.py:15
  235.0 0.0 copy-start.1
  235.0 9.4 copy.20
  244.5 0.0 copy-done.1
  244.5 0.1 dynamic_slice.6
  244.6 0.3 select_bitcast_fusion.1
  244.9 7.0 fusion.26
  251.9 6.4 slice_bitcast_fusion.1
  258.3 65.5 %fusion.8 = f32[64,128,8,256]{1,3,2,0:T(8,128)} fusion(f32[64,128,256,1]{2,0,1,3:T(8,128)} %get-tuple-element.10, f32[64,128,1024]{2,1,0:T(8,128)} %param.5), kind=kOutput, calls=%fused_computation.9 | convolution fusion | flops 25769803776 | bytes 109051904 | tf_op jit(solution)/shard_map/emnj,ejd->emnd/dot_general | solution.py:72
  323.8 38.4 %slice.46 = f32[64,128,7,256]{1,3,2,0:T(8,128)} slice(f32[64,128,8,256]{1,3,2,0:T(8,128)} %fusion.8), slice={[0:64], [0:128], [1:8], [0:256]} | slice | bytes 117440512 | tf_op jit(solution)/shard_map/slice | solution.py:76
  362.2 88.9 %bitcast_add_fusion = f32[64,128,8,256]{1,3,2,0:T(8,128)} fusion(f32[64,128,7,256]{1,3,2,0:T(8,128)} %slice.46, f32[64,128,256,1]{2,0,1,3:T(8,128)} %get-tuple-element.9, f32[64,128,1024]{2,1,0:T(8,128)} %param.5), kind=kOutput, calls=%fused_computation.2 | convolution fusion | flops 25786580992 | bytes 167772160 | tf_op jit(solution)/shard_map/emnj,ejd->emnd/dot_general | solution.py:69
  451.1 8.4 fusion.32
  459.5 113.8 %fusion.18 = f32[512,64,128]{2,0,1:T(8,128)} fusion(f32[64,128,2048]{1,2,0:T(8,128)} %bitcast.13, f32[2048,256]{0,1:T(8,128)S(1)} %get-tuple-element.14, f32[2048,256]{0,1:T(8,128)S(1)} %get-tuple-element.13), kind=kOutput, calls=%fused_computation.23 | convolution fusion | flops 103081312256 | bytes 88080384 | tf_op jit(solution)/shard_map/dot_general | solution.py:80
  573.3 11.1 %fusion.102 = (f32[256,64,128]{2,0,1:T(8,128)}, f32[256,64,128]{2,0,1:T(8,128)}) fusion(f32[512,64,128]{2,0,1:T(8,128)} %fusion.18), kind=kLoop, calls=%fused_computation.140 | loop fusion | bytes 33554432 | tf_op jit(solution)/shard_map/slice | solution.py:46
  584.4 34.5 %fusion.13 = f32[256,64,256]{2,1,0:T(8,128)} fusion(f32[256,128,256]{2,1,0:T(8,128)} %param.9, f32[256,64,128]{2,0,1:T(8,128)} %get-tuple-element.8), kind=kOutput, calls=%fused_computation.17 | convolution fusion | flops 6442450944 | bytes 58720256 | tf_op jit(solution)/shard_map/dot_general | solution.py:50
  618.9 34.9 %fusion.15 = f32[256,64,256]{2,1,0:T(8,128)} fusion(f32[256,128,256]{2,1,0:T(8,128)} %param.9, f32[256,64,128]{2,0,1:T(8,128)} %get-tuple-element.7), kind=kOutput, calls=%fused_computation.19 | convolution fusion | flops 6442450944 | bytes 58720256 | tf_op jit(solution)/shard_map/dot_general | solution.py:49
  653.9 18.7 %slice_subtract_fusion = (f32[256,64,128]{2,1,0:T(8,128)}, f32[256,64,128]{2,1,0:T(8,128)}) fusion(f32[256,64,256]{2,1,0:T(8,128)} %fusion.13, f32[256,64,256]{2,1,0:T(8,128)} %fusion.15), kind=kLoop, calls=%fused_computation.12 | loop fusion | flops 4194304 | bytes 50331648 | tf_op jit(solution)/shard_map/sub | solution.py:52
  672.6 11.5 %pad_maximum_fusion = f32[256,64,256]{2,1,0:T(8,128)} fusion(f32[256,64,128]{2,1,0:T(8,128)} %get-tuple-element.6, f32[256,64,128]{2,1,0:T(8,128)} %get-tuple-element.5), kind=kLoop, calls=%fused_computation.10 | loop fusion | flops 4194304 | bytes 33554432 | tf_op jit(solution)/shard_map/concatenate | solution.py:51
  684.1 0.0 copy-start
  684.1 0.0 reduce-scatter.2.cloned.1.call-update
  684.1 0.2 all-gather.2.cloned.1.call-start
  684.3 118.8 %reduce-scatter.2.cloned.1.call-done = f32[32,64,256]{2,1,0:T(8,128)} async-done(((f32[256,64,256]{2,1,0:T(8,128)}), f32[32,64,256]{2,1,0:T(8,128)}) %reduce-scatter.2.cloned.1.call-update) | async-done | bytes 2097168 | tf_op jit(solution)/shard_map/reduce_scatter | solution.py:85
  803.2 0.0 all-gather.2.cloned.1.call-update
  803.2 0.0 copy-done
  803.3 151.1 %all-gather.2.cloned.1.call-done = f32[32,256,256]{2,1,0:T(8,128)} async-done(((f32[32,64,256]{2,1,0:T(8,128)}), f32[32,256,256]{2,1,0:T(8,128)}) %all-gather.2.cloned.1.call-update) | async-done | bytes 8388624 | tf_op jit(solution)/shard_map/all_gather | solution.py:92
  954.4 10.3 %convolution_bitcast_fusion = f32[32,64,256]{2,1,0:T(8,128)} fusion(f32[32,256,256]{2,1,0:T(8,128)} %all-gather.2.cloned.1.call-done, s32[64]{0:T(128)S(1)} %get-tuple-element.26, s32[256]{0:T(256)S(1)} %get-tuple-element.24, s32[64]{0:T(128)S(1)} %get-tuple-element.27, s32[256]{0:T(256)S(1)} %get-tuple-element.25, s32[64]{0:T(128)S(1)} %get-tuple-element.28, ...), kind=kOutput, calls=%fused_computation.36 | convolution fusion | flops 1611284480 | bytes 10497280 | tf_op jit(solution)/shard_map/dot_general | solution.py:91
  (10 shorter events, 0.1 us)
Async XLA Ops:
  6.5 796.6 %reduce-scatter.2.cloned.1.call-start = ((), (), s32[]{:S(2)}) async-start(), calls=%async_computation.1 | async-start | bytes 18874368 | tf_op jit(solution)/shard_map/reduce_scatter | solution.py:85
  235.0 9.4 copy-start.1
  684.1 119.2 %copy-start = (s32[256]{0:T(256)S(1)}, s32[256]{0:T(256)}, u32[]{:S(2)}) copy-start(s32[256]{0:T(256)} %param.8) | copy-start | bytes 3076
  684.1 270.3 %all-gather.2.cloned.1.call-start = ((), (), s32[]{:S(2)}) async-start(), calls=%async_computation.2 | async-start | bytes 10485760 | tf_op jit(solution)/shard_map/all_gather | solution.py:92
Sparse Core Ops, SparseCore 0:
  684.2 118.8 reduce-scatter.1
  804.7 149.6 all-gather.1
where the time goes:
time: 979 us; the launch traced here: 972 us
  matrix products  355 us (36%)
  local copies, waits for them, and re-layouts  294 us (30%)
  waiting for transfers between devices  270 us (28%)
  other arithmetic  39.1 us (4%)
  between operations  13.7 us (1%)
    all_gather x1, waiting for transfers between devices, per_device(): lax.all_gather(coded, 'emit', axis=1, tiled=True)  151 us
    reduce_scatter x1, waiting for transfers between devices, per_device(): lax.psum_scatter(steer_bins(spectra, steer, bins_dev * lax.axis_size('ele...  119 us
    gather x2, local copies, waits for them, and re-layouts, toeplitz_table(): quadrature = jnp.where(inside[None], codes[:, 1, :][:, clipped], 0.0)  118 us
    gather x2, local copies, waits for them, and re-layouts, toeplitz_table(): in_phase = jnp.where(inside[None], codes[:, 0, :][:, clipped], 0.0)  118 us
    dot_general x1, matrix products, per_device(): lax.dot_general(transform, corr, (((0,), (2,)), ((), ())), precision=lax....  114 us
    dot_general x1, matrix products, per_device(): jnp.einsum('emnj,ejd->emnd', blocks, picked[:, :taps, :], precision=lax.P...  88.9 us
    dot_general x1, matrix products, per_device(): jnp.einsum('emnj,ejd->emnd', blocks, picked[:, taps:, :], precision=lax.P...  65.5 us
    slice x1, local copies, waits for them, and re-layouts, per_device(): following[:, :, 1:]  38.4 us
  transfers between devices with their start and end apart: 2, of which 2 were waited for; matrix products, arithmetic and copies ran while one was open for 0% of the time, Pallas kernels for 0%

commit v1 on v0

--- a/solution.py
+++ b/solution.py
@@ -2,6 +2,28 @@
 import jax.numpy as jnp
 from jax import lax
 from jax.sharding import PartitionSpec as P
+
+
+def laid_out(parts, dim):
+    parts = jnp.moveaxis(parts, 0, dim)
+    shape = parts.shape
+    return parts.reshape(*shape[:dim], shape[dim] * shape[dim + 1], *shape[dim + 2 :])
+
+
+def collected_by_bits(array, axis):
+    size = lax.axis_size(axis)
+    blocks = array[None]
+    for level in range(size.bit_length() - 1):
+        apart = 1 << level
+        other = lax.ppermute(blocks, axis, [(i, i ^ apart) for i in range(size)])
+        both = jnp.stack([blocks, other])
+        upper = lax.axis_index(axis) >> level & 1
+        blocks = jnp.where(upper == 0, both, both[::-1]).reshape(-1, *array.shape)
+    return blocks
+
+
+def collect(array, axis, dim):
+    return laid_out(collected_by_bits(array, axis), dim)
 
 
 def toeplitz_table(codes):
@@ -89,7 +111,7 @@
         tiled=True,
     )
     folded = lax.dot_general(
-        lax.all_gather(coded, "emit", axis=1, tiled=True),
+        collect(coded, "emit", 1),
         hadamard,
         (((1,), (0,)), ((), ())),
         precision=lax.Precision.HIGHEST,

time: 979 us -> 1070 us (1.093)
  waiting for transfers between devices: 270 us -> 345 us
  other arithmetic: 39.1 us -> 51.5 us
    ppermute x0 -> x2, waiting for transfers between devices: none -> 226 us  [collected_by_bits(): other = lax.ppermute(blocks, axis, [(i, i ^ apart) for i in range(size)])]
    all_gather x1 -> x0, waiting for transfers between devices: 151 us -> none  [per_device(): lax.all_gather(coded, 'emit', axis=1, tiled=True)]
  transfers between devices with their start and end apart: 2 -> 3, of which waited for: 2 -> 3; matrix products, arithmetic and copies ran while one was open for 0% -> 0% of each run, Pallas kernels for 0% -> 0%
where the time goes in v1:
time: 1070 us; the launch traced here: 1060 us
  matrix products  352 us (33%)
  waiting for transfers between devices  345 us (32%)
  local copies, waits for them, and re-layouts  295 us (28%)
  other arithmetic  51.5 us (5%)
  between operations  13.8 us (1%)
    ppermute x2, waiting for transfers between devices, collected_by_bits(): other = lax.ppermute(blocks, axis, [(i, i ^ apart) for i in range(size)])  226 us
    reduce_scatter x1, waiting for transfers between devices, per_device(): lax.psum_scatter(steer_bins(spectra, steer, bins_dev * lax.axis_size('ele...  119 us
    gather x2, local copies, waits for them, and re-layouts, toeplitz_table(): quadrature = jnp.where(inside[None], codes[:, 1, :][:, clipped], 0.0)  118 us
    gather x2, local copies, waits for them, and re-layouts, toeplitz_table(): in_phase = jnp.where(inside[None], codes[:, 0, :][:, clipped], 0.0)  118 us
    dot_general x1, matrix products, per_device(): lax.dot_general(transform, corr, (((0,), (2,)), ((), ())), precision=lax....  114 us
    dot_general x1, matrix products, per_device(): jnp.einsum('emnj,ejd->emnd', blocks, picked[:, :taps, :], precision=lax.P...  88.9 us
    dot_general x1, matrix products, per_device(): jnp.einsum('emnj,ejd->emnd', blocks, picked[:, taps:, :], precision=lax.P...  65.5 us
    slice x1, local copies, waits for them, and re-layouts, per_device(): following[:, :, 1:]  38.4 us
  transfers between devices with their start and end apart: 3, of which 3 were waited for; matrix products, arithmetic and copies ran while one was open for 0% of the time, Pallas kernels for 0%

profile of v1, /device:TPU:0, one launch (start us, length us, event | category | flops | bytes accessed | tf_op | source)
XLA Modules:
  0.0 1060.5 jit_solution(1244423147068834479)
XLA Ops:
  6.5 0.0 reduce-scatter.2.cloned.1.call-start
  6.5 0.1 fusion.36
  6.7 0.8 fusion.105
  7.5 0.1 copy.41
  7.6 109.0 %gather_fusion = f32[32768,4]{1,0:T(8,128)} fusion(f32[4,128]{0,1:T(8,128)S(1)} %bitcast.78, s32[32768]{0:T(1024)S(1)} %fusion.36), kind=kCustom, calls=%fused_computation | custom fusion | bytes 1179648 | tf_op jit(solution)/shard_map/gather | solution.py:36
  116.5 9.4 copy.18
  126.0 0.1 copy.42
  126.1 109.0 %gather_fusion.1 = f32[32768,4]{1,0:T(8,128)} fusion(f32[4,128]{0,1:T(8,128)S(1)} %bitcast.77, s32[32768]{0:T(1024)S(1)} %fusion.36), kind=kCustom, calls=%fused_computation.1 | custom fusion | bytes 1179648 | tf_op jit(solution)/shard_map/gather | solution.py:37
  235.0 0.0 copy-start.1
  235.0 9.4 copy.21
  244.5 0.0 copy-done.1
  244.5 0.1 dynamic_slice.6
  244.6 0.3 select_bitcast_fusion.1
  244.9 7.0 fusion.28
  251.9 6.4 slice_bitcast_fusion.1
  258.3 65.5 %fusion.8 = f32[64,128,8,256]{1,3,2,0:T(8,128)} fusion(f32[64,128,256,1]{2,0,1,3:T(8,128)} %get-tuple-element.10, f32[64,128,1024]{2,1,0:T(8,128)} %param.5), kind=kOutput, calls=%fused_computation.9 | convolution fusion | flops 25769803776 | bytes 109051904 | tf_op jit(solution)/shard_map/emnj,ejd->emnd/dot_general | solution.py:94
  323.8 38.4 %slice.46 = f32[64,128,7,256]{1,3,2,0:T(8,128)} slice(f32[64,128,8,256]{1,3,2,0:T(8,128)} %fusion.8), slice={[0:64], [0:128], [1:8], [0:256]} | slice | bytes 117440512 | tf_op jit(solution)/shard_map/slice | solution.py:98
  362.2 88.9 %bitcast_add_fusion = f32[64,128,8,256]{1,3,2,0:T(8,128)} fusion(f32[64,128,7,256]{1,3,2,0:T(8,128)} %slice.46, f32[64,128,256,1]{2,0,1,3:T(8,128)} %get-tuple-element.9, f32[64,128,1024]{2,1,0:T(8,128)} %param.5), kind=kOutput, calls=%fused_computation.2 | convolution fusion | flops 25786580992 | bytes 167772160 | tf_op jit(solution)/shard_map/emnj,ejd->emnd/dot_general | solution.py:91
  451.1 8.4 fusion.34
  459.5 113.8 %fusion.18 = f32[512,64,128]{2,0,1:T(8,128)} fusion(f32[64,128,2048]{1,2,0:T(8,128)} %bitcast.13, f32[2048,256]{0,1:T(8,128)S(1)} %get-tuple-element.16, f32[2048,256]{0,1:T(8,128)S(1)} %get-tuple-element.15), kind=kOutput, calls=%fused_computation.26 | convolution fusion | flops 103081312256 | bytes 88080384 | tf_op jit(solution)/shard_map/dot_general | solution.py:102
  573.3 11.1 %fusion.104 = (f32[256,64,128]{2,0,1:T(8,128)}, f32[256,64,128]{2,0,1:T(8,128)}) fusion(f32[512,64,128]{2,0,1:T(8,128)} %fusion.18), kind=kLoop, calls=%fused_computation.146 | loop fusion | bytes 33554432 | tf_op jit(solution)/shard_map/slice | solution.py:68
  584.4 34.5 %fusion.13 = f32[256,64,256]{2,1,0:T(8,128)} fusion(f32[256,128,256]{2,1,0:T(8,128)} %param.9, f32[256,64,128]{2,0,1:T(8,128)} %get-tuple-element.8), kind=kOutput, calls=%fused_computation.19 | convolution fusion | flops 6442450944 | bytes 58720256 | tf_op jit(solution)/shard_map/dot_general | solution.py:72
  618.9 34.9 %fusion.15 = f32[256,64,256]{2,1,0:T(8,128)} fusion(f32[256,128,256]{2,1,0:T(8,128)} %param.9, f32[256,64,128]{2,0,1:T(8,128)} %get-tuple-element.7), kind=kOutput, calls=%fused_computation.21 | convolution fusion | flops 6442450944 | bytes 58720256 | tf_op jit(solution)/shard_map/dot_general | solution.py:71
  653.9 18.7 %slice_subtract_fusion = (f32[256,64,128]{2,1,0:T(8,128)}, f32[256,64,128]{2,1,0:T(8,128)}) fusion(f32[256,64,256]{2,1,0:T(8,128)} %fusion.13, f32[256,64,256]{2,1,0:T(8,128)} %fusion.15), kind=kLoop, calls=%fused_computation.13 | loop fusion | flops 4194304 | bytes 50331648 | tf_op jit(solution)/shard_map/sub | solution.py:74
  672.6 11.7 %pad_maximum_fusion = f32[256,64,256]{2,1,0:T(8,128)} fusion(f32[256,64,128]{2,1,0:T(8,128)} %get-tuple-element.6, f32[256,64,128]{2,1,0:T(8,128)} %get-tuple-element.5), kind=kLoop, calls=%fused_computation.10 | loop fusion | flops 4194304 | bytes 33554432 | tf_op jit(solution)/shard_map/concatenate | solution.py:73
  684.2 0.0 reduce-scatter.2.cloned.1.call-update
  684.3 119.0 %reduce-scatter.2.cloned.1.call-done = f32[32,64,256]{2,1,0:T(8,128)} async-done(((f32[256,64,256]{2,1,0:T(8,128)}), f32[32,64,256]{2,1,0:T(8,128)}) %reduce-scatter.2.cloned.1.call-update) | async-done | bytes 2097168 | tf_op jit(solution)/shard_map/reduce_scatter | solution.py:107
  803.3 1.5 collective-permute-start
  804.8 45.9 %collective-permute-done = f32[1,32,64,256]{3,2,1,0:T(8,128)S(1)} collective-permute-done((f32[1,32,64,256]{3,2,1,0:T(8,128)}, f32[1,32,64,256]{3,2,1,0:T(8,128)S(1)}, u32[]{:S(2)}, u32[]{:S(2)}) %collective-permute-start) | collective-permute-done | bytes 2097184 | tf_op jit(solution)/shard_map/ppermute | solution.py:18
  850.7 2.0 pad_maximum_fusion.2
  852.7 0.0 copy-start
  852.7 4.6 fusion.23
  857.3 2.4 collective-permute-start.1
  859.8 0.0 copy-done
  859.8 179.9 %collective-permute-done.1 = f32[2,32,64,256]{3,2,1,0:T(8,128)} collective-permute-done((f32[2,32,64,256]{3,2,1,0:T(8,128)}, f32[2,32,64,256]{3,2,1,0:T(8,128)}, u32[]{:S(2)}, u32[]{:S(2)}) %collective-permute-start.1) | collective-permute-done | bytes 4194336 | tf_op jit(solution)/shard_map/ppermute | solution.py:18
  1039.7 4.1 pad_maximum_fusion.1
  1043.8 1.6 reverse_select_fusion
  1045.5 1.1 copy.29
  1046.6 6.9 convolution_bitcast_fusion
  (10 shorter events, 0.1 us)
Async XLA Ops:
  6.5 796.8 %reduce-scatter.2.cloned.1.call-start = ((), (), s32[]{:S(2)}) async-start(), calls=%async_computation.1 | async-start | bytes 18874368 | tf_op jit(solution)/shard_map/reduce_scatter | solution.py:107
  235.0 9.4 copy-start.1
  803.3 47.4 %collective-permute-start = (f32[1,32,64,256]{3,2,1,0:T(8,128)}, f32[1,32,64,256]{3,2,1,0:T(8,128)S(1)}, u32[]{:S(2)}, u32[]{:S(2)}) collective-permute-start(f32[1,32,64,256]{3,2,1,0:T(8,128)} %bitcast.83), channel_id=1, source_target_pairs={{0,8},{8,0},{16,24},{24,16},{1,9},{9,1},{17,25},{25,17},{2,10},{10... | collective-permute-start | bytes 6291464 | tf_op jit(solution)/shard_map/ppermute | solution.py:18
  852.7 7.0 copy-start
  857.3 182.4 %collective-permute-start.1 = (f32[2,32,64,256]{3,2,1,0:T(8,128)}, f32[2,32,64,256]{3,2,1,0:T(8,128)}, u32[]{:S(2)}, u32[]{:S(2)}) collective-permute-start(f32[2,32,64,256]{3,2,1,0:T(8,128)} %get-tuple-element.12), channel_id=1, source_target_pairs={{0,16},{8,24},{16,0},{24,8},{1,17},{9,25},{17,1},{25,9},{2,18},{10... | collective-permute-start | bytes 12582920 | tf_op jit(solution)/shard_map/ppermute | solution.py:18
Sparse Core Ops, SparseCore 0:
  684.4 118.8 reduce-scatter.1
